TPU v7x, 32 devices: a whole 2x2x4 slice. The times are simulated.
32 devices in a mesh: groups: 2 (over y), gx: 4 (over z), gy: 2 (over x), gz: 2 (over core).
Axes of the slice: x: 2, y: 2, z: 4, core: 2. Of those that a mesh axis runs over, the one named last changes fastest.
Arguments:
- polar_angle: float32 [16, 512, 256], P('gz', ('groups', 'gx'), 'gy'), parts along dimension 1, may hold values from -3.140625 to 3.140625
- azimuth: float32 [16, 512, 256], P('gz', ('groups', 'gx'), 'gy'), parts along dimension 1, may hold values from -3.140625 to 3.140625
- classes: int32 [6, 16, 512, 256], P(None, 'gz', ('groups', 'gx'), 'gy'), parts along dimension 2, may hold values from 0 to 7, as said below
- exchange_table: float32 [8], replicated, may hold values from 0.3 to 1.5
Outputs:
- spins_final: float32 [3, 16, 512, 256], P(None, 'gz', ('groups', 'gx'), 'gy'), parts along dimension 2
- modes_mid: float32 [32, 6144], P(('groups', 'gx')), parts along dimension 0
- modes_end: float32 [32, 6144], P(('groups', 'gx')), parts along dimension 0
There are 2 independent parts, one for each index of `groups`. A program takes and returns all parts, laid end to end along the dimension named above; an argument that names none is the same for every part. Nothing has to cross between parts.
Inputs may be any that keep to these rules, and one draw needn't show every extreme that they name: `classes`: entry 3 + d of a site equals entry d of its lower neighbour along direction d (periodically), so every bond has one class seen from both ends.
All inputs are finite; a program needn't handle non-finite values.
Results may differ from a plain program's by a relative error of at most 0.0001.
Values sent between devices are 32-bit elements; how exact they have to be, the bound alone decides.
A program may use at most 128 MiB of HBM per device.

v0:
```python
import functools
import math

import jax
import jax.numpy as jnp
from jax import lax
from jax.experimental import pallas as pl
from jax.experimental.pallas import tpu as pltpu
from jax.sharding import PartitionSpec as P

KX = 32
KY = 32
STEPS = 4
HALO = 8
MESH = pl.DeviceIdType.MESH

time_step = 0.1
damping = 0.1


def sin_cos(angle):
    turns = jnp.floor(angle * (2.0 / math.pi) + 0.5)
    rest = angle - turns * 1.5703125
    rest = rest - turns * 4.837512969970703125e-4
    rest = rest - turns * 7.54978995489188216e-8
    square = rest * rest
    sine = rest + rest * square * (
        -1.6666654611e-1 + square * (8.3321608736e-3 + square * -1.9515295891e-4)
    )
    cosine = (1.0 - 0.5 * square) + square * square * (
        4.166664568298827e-2 + square * (-1.388731625493765e-3 + square * 2.443315711809948e-5)
    )
    size = jnp.abs(turns)
    odd = size == 1.0
    half = size == 2.0
    sine_out = jnp.where(odd, jnp.where(turns > 0.0, cosine, -cosine), jnp.where(half, -sine, sine))
    cosine_out = jnp.where(odd, jnp.where(turns > 0.0, -sine, sine), jnp.where(half, -cosine, cosine))
    return sine_out, cosine_out


def spins_of(polar, azimuth):
    sine_polar, cosine_polar = sin_cos(polar)
    sine_azimuth, cosine_azimuth = sin_cos(azimuth)
    return sine_polar * cosine_azimuth, sine_polar * sine_azimuth, cosine_polar


def lookup(classes, table_ref):
    values = [table_ref[i] for i in range(table_ref.shape[0])]
    bit = 1
    level = None
    while len(values) > 1:
        mask = (classes & bit) != 0
        values = [
            jnp.where(mask, values[i + 1], values[i]) if i + 1 < len(values) else values[i]
            for i in range(0, len(values), 2)
        ]
        bit *= 2
    return values[0] + jnp.zeros(classes.shape, jnp.float32)


def velocity_of(spin, field):
    s0, s1, s2 = spin
    h0, h1, h2 = field
    t0 = s1 * h2 - s2 * h1
    t1 = s2 * h0 - s0 * h2
    t2 = s0 * h1 - s1 * h0
    return (
        -t0 - damping * (s1 * t2 - s2 * t1),
        -t1 - damping * (s2 * t0 - s0 * t2),
        -t2 - damping * (s0 * t1 - s1 * t0),
    )


def evolve_kernel(sizes, polar_ref, azimuth_ref, classes_ref, table_ref, mid_ref, end_ref,
                  S, Q, J, GS, GQ, GJ, OS, OQ, ins, low, high, lowk, highk,
                  pack, left_pack, right_pack,
                  xs, xr, ys, yr, zs, zr, gs, gr, osem):
    nx, ny, nz = sizes
    depth, wide, lanes = polar_ref.shape
    ext = wide + 2 * HALO
    tiles = ext // 8
    inner = wide // 8
    group = 2 * HALO
    me_x, me_y, me_z = lax.axis_index("gx"), lax.axis_index("gy"), lax.axis_index("gz")

    def at(axis, me, n, step):
        return {axis: lax.rem(me + (step + n), n)}

    x_left, x_right = at("gx", me_x, nx, -1), at("gx", me_x, nx, 1)
    y_left, y_right = at("gy", me_y, ny, -1), at("gy", me_y, ny, 1)
    z_down, z_up = at("gz", me_z, nz, -1), at("gz", me_z, nz, 1)

    barrier = pltpu.get_barrier_semaphore()
    for who in (x_left, x_right, y_left, y_right, z_down, z_up):
        pl.semaphore_signal(barrier, inc=1, device_id=who, device_id_type=MESH)
    pl.semaphore_wait(barrier, 6)

    def remote(src, dst, send, recv, who):
        return pltpu.make_async_remote_copy(
            src_ref=src, dst_ref=dst, send_sem=send, recv_sem=recv, device_id=who, device_id_type=MESH
        )

    top = pl.ds(wide - HALO, HALO)
    bottom = pl.ds(0, HALO)
    x_copies = [
        remote(polar_ref.at[:, top, :], low.at[0], xs.at[0], xr.at[0], x_right),
        remote(azimuth_ref.at[:, top, :], low.at[1], xs.at[1], xr.at[1], x_right),
        remote(classes_ref.at[:, :, top, :], lowk, xs.at[2], xr.at[2], x_right),
        remote(polar_ref.at[:, bottom, :], high.at[0], xs.at[3], xr.at[3], x_left),
        remote(azimuth_ref.at[:, bottom, :], high.at[1], xs.at[4], xr.at[4], x_left),
        remote(classes_ref.at[:, :, bottom, :], highk, xs.at[5], xr.at[5], x_left),
    ]
    for copy in x_copies:
        copy.start()

    lane = lax.broadcasted_iota(jnp.int32, (8, lanes), 1)
    group_of = lane // group
    place = lane % group

    def spread(z, polar, azimuth, classes_at, row):
        where_to = pl.ds(row, 8)
        shift = group * z + HALO
        mine = group_of == z
        spin = spins_of(polar, azimuth)
        for c in range(3):
            S[c, z + 1, where_to, :] = spin[c]
            old = pack[c, where_to, :]
            pack[c, where_to, :] = jnp.where(mine, pltpu.roll(spin[c], shift, 1), old)
        for d in range(6):
            value = lookup(classes_at(d), table_ref)
            J[d, z, where_to, :] = value
            old = pack[3 + d, where_to, :]
            pack[3 + d, where_to, :] = jnp.where(mine, pltpu.roll(value, shift, 1), old)

    pack[...] = jnp.zeros(pack.shape, jnp.float32)

    def own(z, carry):
        for r in range(inner):
            rows = pl.ds(8 * r, 8)
            spread(z, polar_ref[z, rows, :], azimuth_ref[z, rows, :],
                   lambda d: classes_ref[d, z, rows, :], HALO + 8 * r)
        return carry

    lax.fori_loop(0, depth, own, 0)

    def y_copies(part):
        rows = (pl.ds(HALO, wide), pl.ds(0, HALO), pl.ds(HALO + wide, HALO))[part]
        made = [remote(pack.at[:, rows, :], left_pack.at[:, rows, :], ys.at[part], yr.at[part], y_right)]
        if ny > 2:
            made.append(remote(pack.at[:, rows, :], right_pack.at[:, rows, :], ys.at[3 + part], yr.at[3 + part], y_left))
        return made

    def z_copies(field, base):
        return [
            remote(field.at[:, 1], field.at[:, depth + 1], zs.at[base], zr.at[base], z_down),
            remote(field.at[:, depth], field.at[:, 0], zs.at[base + 1], zr.at[base + 1], z_up),
        ]

    def g_copy(ghost, other, base):
        return remote(ghost, other, gs.at[base], gr.at[base], z_up)

    for copy in y_copies(0):
        copy.start()
    for copy in x_copies:
        copy.wait()

    def edges(z, carry):
        spread(z, low[0, z], low[1, z], lambda d: lowk[d, z], 0)
        spread(z, high[0, z], high[1, z], lambda d: highk[d, z], HALO + wide)
        return carry

    lax.fori_loop(0, depth, edges, 0)
    for part in (1, 2):
        for copy in y_copies(part):
            copy.start()
    for copy in z_copies(S, 0):
        copy.start()
    for part in range(3):
        for copy in y_copies(part):
            copy.wait()
    from_right = left_pack if ny == 2 else right_pack

    def ghosts(r, carry):
        rows = pl.ds(pl.multiple_of(8 * r, 8), 8)
        for f in range(9):
            value = jnp.where(place < HALO, left_pack[f, rows, :], from_right[f, rows, :])
            if f < 3:
                GS[f, rows, :] = value
            else:
                GJ[f - 3, rows, :] = value
        return carry

    lax.fori_loop(0, tiles, ghosts, 0)
    g_copy(GS, OS, 0).start()

    def x_pair(ref, r, value):
        if r < tiles - 1:
            ahead = ref[pl.ds(8 * r + 1, 8), :]
        else:
            ahead = pltpu.roll(value, 7, 0)
        if r > 0:
            behind = ref[pl.ds(8 * r - 1, 8), :]
        else:
            behind = pltpu.roll(value, 1, 0)
        return ahead, behind

    def plane(F, G, z, finish):
        up_shift = lanes - (group * z + HALO)
        left_mask = lane == group * z + HALO - 1
        right_mask = lane == group * z + HALO
        for r in range(tiles):
            rows = pl.ds(8 * r, 8)
            coupling = [J[d, z, rows, :] for d in range(6)]
            spin, field = [], []
            for c in range(3):
                M = F[c, z + 1, rows, :]
                ahead, behind = x_pair(F.at[c, z + 1], r, M)
                U = pltpu.roll(G[c, rows, :], up_shift, 1)
                right = pltpu.roll(jnp.where(lane == 0, U, M), lanes - 1, 1)
                left = pltpu.roll(jnp.where(lane == lanes - 1, U, M), 1, 1)
                total = coupling[0] * ahead + coupling[1] * right
                total = total + coupling[2] * F[c, z + 2, rows, :]
                total = total + coupling[3] * behind
                total = total + coupling[4] * left
                total = total + coupling[5] * F[c, z, rows, :]
                ins[c, rows, :] = jnp.where(
                    left_mask, pltpu.roll(M, group * z + HALO - 1, 1),
                    jnp.where(right_mask, pltpu.roll(M, group * z + HALO + 1, 1), ins[c, rows, :]))
                spin.append(M)
                field.append(total)
            finish(spin, velocity_of(spin, field), z, rows)

    def ghost_pass(G, other, finish):
        for r in range(tiles):
            rows = pl.ds(8 * r, 8)
            coupling = [GJ[d, rows, :] for d in range(6)]
            spin, field = [], []
            for c in range(3):
                M = G[c, rows, :]
                O = other[c, rows, :]
                I = ins[c, rows, :]
                ahead, behind = x_pair(G.at[c], r, M)
                right = jnp.where(place == HALO - 1, I, pltpu.roll(M, lanes - 1, 1))
                left = jnp.where(place == HALO, I, pltpu.roll(M, 1, 1))
                above = pltpu.roll(jnp.where(lane >= group, M, O), lanes - group, 1)
                below = pltpu.roll(jnp.where(lane < lanes - group, M, O), group, 1)
                total = coupling[0] * ahead + coupling[1] * right
                total = total + coupling[2] * above
                total = total + coupling[3] * behind
                total = total + coupling[4] * left
                total = total + coupling[5] * below
                spin.append(M)
                field.append(total)
            finish(spin, velocity_of(spin, field), rows)

    def predict(spin, speed, z, rows):
        for c in range(3):
            Q[c, z + 1, rows, :] = spin[c] + time_step * speed[c]

    def predict_ghost(spin, speed, rows):
        for c in range(3):
            GQ[c, rows, :] = spin[c] + time_step * speed[c]

    def correct(spin, speed, z, rows):
        for c in range(3):
            S[c, z + 1, rows, :] = 0.5 * (S[c, z + 1, rows, :] + spin[c]) + 0.5 * time_step * speed[c]

    def correct_ghost(spin, speed, rows):
        for c in range(3):
            GS[c, rows, :] = 0.5 * (GS[c, rows, :] + spin[c]) + 0.5 * time_step * speed[c]

    ins[...] = jnp.zeros(ins.shape, jnp.float32)

    def stage(F, G, O, base, finish, finish_ghost, send_main, send_ghost):
        def inside(z, carry):
            plane(F, G, z, finish)
            return carry

        def outside(i, carry):
            plane(F, G, i * (depth - 1), finish)
            return carry

        lax.fori_loop(1, depth - 1, inside, 0)
        for copy in z_copies(F, 2 * base):
            copy.wait()
        lax.fori_loop(0, 2, outside, 0)
        send_main()
        g_copy(G, O, base).wait()
        ghost_pass(G, O, finish_ghost)
        send_ghost()

    def out_copy(target):
        return pltpu.make_async_copy(S.at[:, pl.ds(1, depth), pl.ds(HALO, wide), :], target, osem.at[0])

    def step(turn, carry):
        def send_q():
            for copy in z_copies(Q, 2):
                copy.start()

        def send_s():
            @pl.when(turn < STEPS - 1)
            def _():
                for copy in z_copies(S, 0):
                    copy.start()

        def send_gs():
            @pl.when(turn < STEPS - 1)
            def _():
                g_copy(GS, OS, 0).start()

        stage(S, GS, OS, 0, predict, predict_ghost, send_q, lambda: g_copy(GQ, OQ, 1).start())

        @pl.when(turn == 2)
        def _():
            out_copy(mid_ref).wait()

        stage(Q, GQ, OQ, 1, correct, correct_ghost, send_s, send_gs)

        @pl.when(turn == 1)
        def _():
            out_copy(mid_ref).start()

        return carry

    lax.fori_loop(0, STEPS, step, 0)
    out_copy(end_ref).start()
    out_copy(end_ref).wait()


def evolve(polar_angle, azimuth, classes, exchange_table):
    depth, wide, lanes = polar_angle.shape
    sizes = (lax.axis_size("gx"), lax.axis_size("gy"), lax.axis_size("gz"))
    assert sizes[2] == 2 and depth * 2 * HALO == lanes
    ext = wide + 2 * HALO
    f32 = jnp.float32
    out = jax.ShapeDtypeStruct((3, depth, wide, lanes), f32)
    vmem = pl.BlockSpec(memory_space=pltpu.VMEM)
    anywhere = pl.BlockSpec(memory_space=pl.ANY)
    V = pltpu.VMEM
    D = pltpu.SemaphoreType.DMA
    return pl.pallas_call(
        functools.partial(evolve_kernel, sizes),
        out_shape=(out, out),
        in_specs=[vmem, vmem, vmem, pl.BlockSpec(memory_space=pltpu.SMEM)],
        out_specs=(anywhere, anywhere),
        scratch_shapes=[
            V((3, depth + 2, ext, lanes), f32), V((3, depth + 2, ext, lanes), f32),
            V((6, depth, ext, lanes), f32),
            V((3, ext, lanes), f32), V((3, ext, lanes), f32), V((6, ext, lanes), f32),
            V((3, ext, lanes), f32), V((3, ext, lanes), f32), V((3, ext, lanes), f32),
            V((2, depth, HALO, lanes), f32), V((2, depth, HALO, lanes), f32),
            V((6, depth, HALO, lanes), jnp.int32), V((6, depth, HALO, lanes), jnp.int32),
            V((9, ext, lanes), f32), V((9, ext, lanes), f32), V((9, ext, lanes), f32),
            D((6,)), D((6,)), D((6,)), D((6,)), D((4,)), D((4,)), D((2,)), D((2,)), D((1,)),
        ],
        compiler_params=pltpu.CompilerParams(collective_id=0, has_side_effects=True, vmem_limit_bytes=48 * 1024 * 1024),
        name="evolve",
    )(polar_angle, azimuth, classes, exchange_table)


def phase_table(wave_count, length, total_length, offset):
    position = jnp.arange(length, dtype=jnp.int32) + offset
    numbers = jnp.arange(wave_count, dtype=jnp.int32)
    index = position[:, None] * numbers[None, :] % total_length
    phase = index.astype(jnp.float32) * (2.0 * math.pi / total_length)
    return (jnp.cos(phase), jnp.sin(phase))


def project(spin_field, x_table, y_table, z_cos, z_sin, scale):
    depth, wide_x, wide_y = spin_field.shape[1:]
    along_y = jnp.dot(
        spin_field.reshape(-1, wide_y),
        y_table,
        precision=lax.Precision.HIGHEST,
        preferred_element_type=jnp.float32,
    ).reshape(3, depth, wide_x, 2 * KY)
    along_x = jnp.einsum("czxk,xm->czmk", along_y, x_table, precision=lax.Precision.HIGHEST)
    even_even = along_x[:, :, :KX, :KY]
    even_odd = along_x[:, :, :KX, KY:]
    odd_even = along_x[:, :, KX:, :KY]
    odd_odd = along_x[:, :, KX:, KY:]
    cosine_part = even_even - odd_odd
    sine_part = odd_even + even_odd
    hp = lax.Precision.HIGHEST
    real_part = jnp.einsum("czab,zk->kcab", cosine_part, z_cos, precision=hp) - jnp.einsum(
        "czab,zk->kcab", sine_part, z_sin, precision=hp
    )
    imag_part = -(
        jnp.einsum("czab,zk->kcab", sine_part, z_cos, precision=hp)
        + jnp.einsum("czab,zk->kcab", cosine_part, z_sin, precision=hp)
    )
    stacked = jnp.stack([real_part, imag_part], 1) * scale
    return stacked.reshape(z_cos.shape[1], -1)


def reduce_modes(partial_value):
    blocks = lax.psum_scatter(partial_value, "gx", scatter_dimension=0, tiled=True)
    return lax.psum(blocks, ("gy", "gz"))


def body(polar_angle, azimuth, classes, exchange_table):
    depth, wide_x, wide_y = polar_angle.shape
    total_x = wide_x * lax.axis_size("gx")
    total_y = wide_y * lax.axis_size("gy")
    total_z = depth * lax.axis_size("gz")
    x_cos, x_sin = phase_table(KX, wide_x, total_x, lax.axis_index("gx") * wide_x)
    y_cos, y_sin = phase_table(KY, wide_y, total_y, lax.axis_index("gy") * wide_y)
    z_cos, z_sin = phase_table(total_z, depth, total_z, lax.axis_index("gz") * depth)
    x_table = jnp.concatenate([x_cos, x_sin], 1)
    y_table = jnp.concatenate([y_cos, y_sin], 1)
    scale = float(total_x * total_y * total_z) ** (-0.5)
    spin_mid, spin_field = evolve(polar_angle, azimuth, classes, exchange_table)
    partial_mid = project(spin_mid, x_table, y_table, z_cos, z_sin, scale)
    partial_end = project(spin_field, x_table, y_table, z_cos, z_sin, scale)
    width = partial_end.shape[1]
    both_modes = reduce_modes(jnp.concatenate([partial_mid, partial_end], 1))
    modes_mid = both_modes[:, :width]
    modes_end = both_modes[:, width:]
    return (spin_field, modes_mid, modes_end)


def solution(mesh):
    return jax.shard_map(
        body,
        mesh=mesh,
        in_specs=(
            P("gz", ("groups", "gx"), "gy"),
            P("gz", ("groups", "gx"), "gy"),
            P(None, "gz", ("groups", "gx"), "gy"),
            P(),
        ),
        out_specs=(
            P(None, "gz", ("groups", "gx"), "gy"),
            P(("groups", "gx"), None),
            P(("groups", "gx"), None),
        ),
        check_vma=False,
    )
```

profile of v0, /device:TPU:0, one launch (start us, length us, event | category | flops | bytes accessed | tf_op | source)
XLA Modules:
  0.0 160.0 jit_solution(2273333457306338587)
XLA Ops:
  7.4 1.4 copy-done
  8.8 0.9 copy-done.1
  9.8 0.9 copy-done.2
  11.4 44.3 %evolve.1 = (f32[3,8,64,128]{3,2,1,0:T(8,128)S(1)}, f32[3,8,64,128]{3,2,1,0:T(8,128)S(1)}) custom-call(f32[8,64,128]{2,1,0:T(8,128)S(1)} %copy-done.1, f32[8,64,128]{2,1,0:T(8,128)S(1)} %copy-done.2, s32[6,8,64,128]{3,2,1,0:T(8,128)S(1)} %copy-done, f32[8]{0:T(128)S(1)} %copy-done.3), custom_call_target="tpu_custom_call" | custom-call | tf_op jit(solution)/shard_map/evolve/pallas_call | solution.py:341
  55.7 0.8 fusion.19
  56.5 0.8 convolution_bitcast_fusion.1
  57.6 1.0 fusion.12
  58.6 1.0 fusion.16
  59.6 1.0 fusion.4
  60.7 1.0 fusion.5
  62.4 0.7 mul.99
  63.1 0.8 fusion.18
  63.9 0.8 convolution_bitcast_fusion
  65.0 1.0 fusion.10
  66.0 1.0 fusion.6
  67.0 1.0 fusion.2
  68.1 1.0 fusion.1
  69.8 0.7 mul.101
  70.6 0.9 pad_maximum_fusion
  72.8 43.7 %all-reduce.6.cloned.1.call-done = f32[16,12288]{1,0:T(8,128)} async-done(((f32[16,12288]{1,0:T(8,128)}), f32[16,12288]{1,0:T(8,128)}) %all-reduce.6.cloned.1.call-update) | async-done | bytes 786448
  116.5 1.7 %constant_dynamic-slice_fusion = f32[4,12288]{1,0:T(4,128)} fusion(f32[16,12288]{1,0:T(8,128)} %all-reduce.6.cloned.1.call-done, u32[]{:T(128)S(6)} %multiply.1), kind=kLoop, calls=%fused_computation.76 | loop fusion | bytes 393220
  118.2 32.4 %all-reduce.4.cloned.1.call-done = f32[4,12288]{1,0:T(4,128)} async-done(((f32[4,12288]{1,0:T(4,128)}), f32[4,12288]{1,0:T(4,128)}) %all-reduce.4.cloned.1.call-update) | async-done | bytes 196624 | tf_op jit(solution)/shard_map/psum | solution.py:398
  150.7 1.6 %fusion.96 = (f32[4,6144]{1,0:T(4,128)}, f32[4,6144]{1,0:T(4,128)}) fusion(f32[4,12288]{1,0:T(4,128)} %all-reduce.4.cloned.1.call-done), kind=kLoop, calls=%fused_computation.116 | loop fusion | bytes 393216 | tf_op jit(solution)/shard_map/slice | solution.py:418
  152.3 0.9 copy.58
  (23 shorter events, 3.5 us)
Async XLA Ops:
  7.2 109.3 %all-reduce.6.cloned.1.call-start = ((), (), s32[]{:S(2)}) async-start(), calls=%async_computation.1 | async-start | bytes 1572864
  7.4 1.4 copy-start
  8.8 0.9 copy-start.1
  9.8 0.9 copy-start.2
  10.7 0.7 copy-start.3
  70.6 1.0 copy-start.4
  71.5 79.1 %all-reduce.4.cloned.1.call-start = ((), (), s32[]{:S(2)}) async-start(), calls=%async_computation | async-start | bytes 393216 | tf_op jit(solution)/shard_map/psum | solution.py:398
Sparse Core Ops, SparseCore 0:
  71.6 44.8 all-reduce.5
  119.4 31.2 all-reduce.3
where the time goes:
time: 160 us
  waiting for transfers between devices  76.1 us (48%)
  Pallas kernels  44.3 us (28%)
  between operations  14.9 us (9%)
  matrix products  11.4 us (7%)
  local copies, waits for them, and re-layouts  11.2 us (7%)
  other arithmetic  2.02 us (1%)
    pallas_call x1, Pallas kernels, evolve(): pl.pallas_call(functools.partial(evolve_kernel, sizes), out_shape=(out, o...  44.3 us
    unnamed x3, waiting for transfers between devices  43.7 us
    psum x1, waiting for transfers between devices, reduce_modes(): return lax.psum(blocks, ('gy', 'gz'))  32.4 us
    unnamed x13, local copies, waits for them, and re-layouts  7.13 us
  transfers between devices with their start and end apart: 2, of which 2 were waited for; matrix products, arithmetic and copies ran while one was open for 0% of the time, Pallas kernels for 0%

commit v1 on v0

--- a/solution.py
+++ b/solution.py
@@ -3,6 +3,7 @@
 
 import jax
 import jax.numpy as jnp
+import numpy as np
 from jax import lax
 from jax.experimental import pallas as pl
 from jax.experimental.pallas import tpu as pltpu
@@ -358,65 +359,150 @@
     )(polar_angle, azimuth, classes, exchange_table)
 
 
-def phase_table(wave_count, length, total_length, offset):
-    position = jnp.arange(length, dtype=jnp.int32) + offset
-    numbers = jnp.arange(wave_count, dtype=jnp.int32)
-    index = position[:, None] * numbers[None, :] % total_length
-    phase = index.astype(jnp.float32) * (2.0 * math.pi / total_length)
-    return (jnp.cos(phase), jnp.sin(phase))
-
-
-def project(spin_field, x_table, y_table, z_cos, z_sin, scale):
-    depth, wide_x, wide_y = spin_field.shape[1:]
-    along_y = jnp.dot(
-        spin_field.reshape(-1, wide_y),
-        y_table,
-        precision=lax.Precision.HIGHEST,
-        preferred_element_type=jnp.float32,
-    ).reshape(3, depth, wide_x, 2 * KY)
-    along_x = jnp.einsum("czxk,xm->czmk", along_y, x_table, precision=lax.Precision.HIGHEST)
-    even_even = along_x[:, :, :KX, :KY]
-    even_odd = along_x[:, :, :KX, KY:]
-    odd_even = along_x[:, :, KX:, :KY]
-    odd_odd = along_x[:, :, KX:, KY:]
-    cosine_part = even_even - odd_odd
-    sine_part = odd_even + even_odd
-    hp = lax.Precision.HIGHEST
-    real_part = jnp.einsum("czab,zk->kcab", cosine_part, z_cos, precision=hp) - jnp.einsum(
-        "czab,zk->kcab", sine_part, z_sin, precision=hp
-    )
-    imag_part = -(
-        jnp.einsum("czab,zk->kcab", sine_part, z_cos, precision=hp)
-        + jnp.einsum("czab,zk->kcab", cosine_part, z_sin, precision=hp)
-    )
-    stacked = jnp.stack([real_part, imag_part], 1) * scale
-    return stacked.reshape(z_cos.shape[1], -1)
-
-
-def reduce_modes(partial_value):
-    blocks = lax.psum_scatter(partial_value, "gx", scatter_dimension=0, tiled=True)
-    return lax.psum(blocks, ("gy", "gz"))
+def phase_table(wave_count, total_length):
+    index = np.arange(total_length)[:, None] * np.arange(wave_count)[None, :] % total_length
+    phase = index * (2.0 * math.pi / total_length)
+    return np.cos(phase).astype(np.float32), np.sin(phase).astype(np.float32)
+
+
+def exact_dot(a, b):
+    return jnp.dot(a, b, precision=lax.Precision.HIGHEST, preferred_element_type=jnp.float32)
+
+
+def modes_kernel(sizes, scale, mid_ref, end_ref, x_ref, y_ref, cos_ref, sin_ref, out_ref,
+                 T, R, Z, D, DR, E, F, zs, zr, xs, xr, ys, yr, fs, fr):
+    nx, ny, nz = sizes
+    depth, wide, lanes = mid_ref.shape[1:]
+    owned = D.shape[1]
+    half = KX // nz
+    me_x, me_y, me_z = lax.axis_index("gx"), lax.axis_index("gy"), lax.axis_index("gz")
+    peers_x = [{"gx": lax.rem(me_x + o, nx)} for o in range(1, nx)]
+    peers_y = [{"gy": lax.rem(me_y + o, ny)} for o in range(1, ny)]
+    twin = {"gz": 1 - me_z}
+
+    barrier = pltpu.get_barrier_semaphore()
+    for who in peers_x + peers_y + [twin]:
+        pl.semaphore_signal(barrier, inc=1, device_id=who, device_id_type=MESH)
+    pl.semaphore_wait(barrier, nx + ny - 1)
+
+    def remote(src, dst, send, recv, who):
+        return pltpu.make_async_remote_copy(
+            src_ref=src, dst_ref=dst, send_sem=send, recv_sem=recv, device_id=who, device_id_type=MESH
+        )
+
+    table = x_ref[...]
+    for c in range(3):
+        for z in range(depth):
+            for turn, ref in enumerate((mid_ref, end_ref)):
+                along_x = exact_dot(table, ref[c, z])
+                T[pl.ds(z * KX, KX), pl.ds(2 * lanes * turn, lanes)] = along_x[:KX]
+                T[pl.ds(z * KX, KX), pl.ds(2 * lanes * turn + lanes, lanes)] = along_x[KX:]
+        parts = exact_dot(T[...], y_ref[...]).reshape(depth, nz, half, 4 * KY)
+        for h in range(nz):
+            R[h, c] = parts[:, h]
+    swap = remote(R.at[1 - me_z], Z, zs.at[0], zr.at[0], twin)
+    swap.start()
+    swap.wait()
+
+    lane = lax.broadcasted_iota(jnp.int32, (half, 4 * KY), 1)
+    cosine_lane = (lane // KY) % 2 == 0
+
+    def waves(block, carry):
+        for c in range(3):
+            ones, twos = [], []
+            for z in range(nz * depth):
+                own = R[me_z, c, z] if z < depth else Z[c, z - depth]
+                ones.append(own)
+                twos.append(jnp.where(cosine_lane, -pltpu.roll(own, 3 * KY, 1), pltpu.roll(own, KY, 1)))
+            for k in range(owned):
+                total = None
+                for z in range(nz * depth):
+                    where_z = me_z * depth + z if z < depth else (1 - me_z) * depth + z - depth
+                    wave = block * owned + k
+                    term = cos_ref[wave, where_z] * ones[z] + sin_ref[wave, where_z] * twos[z]
+                    total = term if total is None else total + term
+                D[block, k, c] = total
+        return carry
+
+    lax.fori_loop(0, nx, waves, 0)
+    x_copies = [
+        remote(D.at[lax.rem(me_x + o, nx)], DR.at[o - 1], xs.at[o - 1], xr.at[o - 1], peers_x[o - 1])
+        for o in range(1, nx)
+    ]
+    for copy in x_copies:
+        copy.start()
+    for copy in x_copies:
+        copy.wait()
+    total = D[me_x]
+    for o in range(1, nx):
+        total = total + DR[o - 1]
+    E[me_y] = total
+    y_copies = [
+        remote(E.at[me_y], E.at[me_y], ys.at[o - 1], yr.at[o - 1], peers_y[o - 1]) for o in range(1, ny)
+    ]
+    for copy in y_copies:
+        copy.start()
+    for copy in y_copies:
+        copy.wait()
+    total = E[0]
+    for o in range(1, ny):
+        total = total + E[o]
+    F[me_z] = total * jnp.where(cosine_lane, scale, -scale)
+    share = remote(F.at[me_z], F.at[me_z], fs.at[0], fr.at[0], twin)
+    share.start()
+    share.wait()
+    out_ref[...] = F[...]
+
+
+def modes(spin_mid, spin_end):
+    depth, wide, lanes = spin_mid.shape[1:]
+    sizes = nx, ny, nz = (lax.axis_size("gx"), lax.axis_size("gy"), lax.axis_size("gz"))
+    total_z = depth * nz
+    owned = total_z // nx
+    half = KX // nz
+    f32 = jnp.float32
+    x_cos, x_sin = phase_table(KX, wide * nx)
+    y_cos, y_sin = phase_table(KY, lanes * ny)
+    z_cos, z_sin = phase_table(total_z, total_z)
+    x_full = np.concatenate([x_cos, x_sin], 1).reshape(nx, wide, 2 * KX).transpose(0, 2, 1)
+    y_pair = np.stack([
+        np.concatenate([y_cos, y_sin], 1).reshape(ny, lanes, 2 * KY),
+        np.concatenate([-y_sin, y_cos], 1).reshape(ny, lanes, 2 * KY),
+    ], 1).reshape(ny, 2 * lanes, 2 * KY)
+    y_full = np.zeros((ny, 4 * lanes, 4 * KY), np.float32)
+    y_full[:, : 2 * lanes, : 2 * KY] = y_pair
+    y_full[:, 2 * lanes :, 2 * KY :] = y_pair
+    x_table = lax.dynamic_index_in_dim(jnp.asarray(x_full), lax.axis_index("gx"), 0, False)
+    y_table = lax.dynamic_index_in_dim(jnp.asarray(y_full), lax.axis_index("gy"), 0, False)
+    scale = float(wide * nx * lanes * ny * total_z) ** -0.5
+    vmem = pl.BlockSpec(memory_space=pltpu.VMEM)
+    smem = pl.BlockSpec(memory_space=pltpu.SMEM)
+    V, DMA = pltpu.VMEM, pltpu.SemaphoreType.DMA
+    width = 4 * KY
+    out = pl.pallas_call(
+        functools.partial(modes_kernel, sizes, scale),
+        out_shape=jax.ShapeDtypeStruct((nz, owned, 3, half, width), f32),
+        in_specs=[vmem, vmem, vmem, vmem, smem, smem],
+        out_specs=vmem,
+        scratch_shapes=[
+            V((depth * KX, 4 * lanes), f32), V((nz, 3, depth, half, width), f32),
+            V((3, depth, half, width), f32), V((nx, owned, 3, half, width), f32),
+            V((nx - 1, owned, 3, half, width), f32), V((ny, owned, 3, half, width), f32),
+            V((nz, owned, 3, half, width), f32),
+            DMA((1,)), DMA((1,)), DMA((nx - 1,)), DMA((nx - 1,)), DMA((ny - 1,)), DMA((ny - 1,)),
+            DMA((1,)), DMA((1,)),
+        ],
+        compiler_params=pltpu.CompilerParams(collective_id=1, has_side_effects=True, vmem_limit_bytes=32 * 1024 * 1024),
+        name="modes",
+    )(spin_mid, spin_end, x_table, y_table, jnp.asarray(z_cos.T), jnp.asarray(z_sin.T))
+    out = out.reshape(nz, owned, 3, half, 2, 2, KY).transpose(4, 1, 5, 2, 0, 3, 6)
+    return out.reshape(2, owned, -1)
 
 
 def body(polar_angle, azimuth, classes, exchange_table):
-    depth, wide_x, wide_y = polar_angle.shape
-    total_x = wide_x * lax.axis_size("gx")
-    total_y = wide_y * lax.axis_size("gy")
-    total_z = depth * lax.axis_size("gz")
-    x_cos, x_sin = phase_table(KX, wide_x, total_x, lax.axis_index("gx") * wide_x)
-    y_cos, y_sin = phase_table(KY, wide_y, total_y, lax.axis_index("gy") * wide_y)
-    z_cos, z_sin = phase_table(total_z, depth, total_z, lax.axis_index("gz") * depth)
-    x_table = jnp.concatenate([x_cos, x_sin], 1)
-    y_table = jnp.concatenate([y_cos, y_sin], 1)
-    scale = float(total_x * total_y * total_z) ** (-0.5)
-    spin_mid, spin_field = evolve(polar_angle, azimuth, classes, exchange_table)
-    partial_mid = project(spin_mid, x_table, y_table, z_cos, z_sin, scale)
-    partial_end = project(spin_field, x_table, y_table, z_cos, z_sin, scale)
-    width = partial_end.shape[1]
-    both_modes = reduce_modes(jnp.concatenate([partial_mid, partial_end], 1))
-    modes_mid = both_modes[:, :width]
-    modes_end = both_modes[:, width:]
-    return (spin_field, modes_mid, modes_end)
+    spin_mid, spin_end = evolve(polar_angle, azimuth, classes, exchange_table)
+    both = modes(spin_mid, spin_end)
+    return (spin_end, both[0], both[1])
 
 
 def solution(mesh):

time: 160 us -> 79 us (0.49)
  waiting for transfers between devices: 76.1 us -> 0 us
  Pallas kernels: 44.3 us -> 68.3 us
  between operations: 14.9 us -> 0.73 us
  matrix products: 11.4 us -> 0 us
  other arithmetic: 2.02 us -> 0 us
  local copies, waits for them, and re-layouts: 11.2 us -> 9.42 us
    unnamed x3 -> x0, waiting for transfers between devices: 43.7 us -> none
    psum x1 -> x0, waiting for transfers between devices: 32.4 us -> none  [reduce_modes(): return lax.psum(blocks, ('gy', 'gz'))]
    pallas_call x0 -> x1, Pallas kernels: none -> 24 us  [modes(): pl.pallas_call(functools.partial(modes_kernel, sizes, scale), out_shape=j...]
    dot_general x12 -> x0, matrix products: 11.4 us -> none  [the longest x2 2.08 us: project(): jnp.einsum('czab,zk->kcab', sine_part, z_sin, precision=hp)]
    squeeze x0 -> x4, local copies, waits for them, and re-layouts: none -> 3.44 us  [the longest x2 1.7 us: body(): return (spin_end, both[0], both[1])]
    mul x4 -> x0, local copies, waits for them, and re-layouts: 2.45 us -> none  [project(): stacked = jnp.stack([real_part, imag_part], 1) * scale]
    unnamed x13, local copies, waits for them, and re-layouts: 7.13 us -> 4.85 us
  transfers between devices with their start and end apart: 2 -> 0, of which waited for: 2 -> 0; matrix products, arithmetic and copies ran while one was open for 0% -> 0% of each run, Pallas kernels for 0% -> 0%
where the time goes in v1:
time: 79 us; the launch traced here: 78.5 us
  Pallas kernels  68.3 us (86%)
  local copies, waits for them, and re-layouts  9.42 us (12%)
    pallas_call x1, Pallas kernels, evolve(): pl.pallas_call(functools.partial(evolve_kernel, sizes), out_shape=(out, o...  44.3 us
    pallas_call x1, Pallas kernels, modes(): pl.pallas_call(functools.partial(modes_kernel, sizes, scale), out_shape=j...  24 us
    unnamed x13, local copies, waits for them, and re-layouts  4.85 us
    squeeze x2, local copies, waits for them, and re-layouts, body(): return (spin_end, both[0], both[1])  1.7 us

profile of v1, /device:TPU:0, one launch (start us, length us, event | category | flops | bytes accessed | tf_op | source)
XLA Modules:
  0.0 78.5 jit_solution(9990492650661259124)
XLA Ops:
  0.6 0.0 copy-start.3
  0.6 0.0 copy-start.4
  0.7 0.8 dynamic-slice_bitcast_fusion.1.x_ref
  1.4 1.0 %dynamic-slice_bitcast_fusion.y_ref = f32[512,128]{1,0:T(8,128)S(1)} fusion(f32[2,512,128]{2,1,0:T(8,128)} %constant.29.clone, s32[]{:T(128)S(6)} %select_n.9), kind=kLoop, calls=%fused_computation | loop fusion | bytes 524292 | tf_op jit(solution)/shard_map/jit(dynamic_index_in_dim)/squeeze | solution.py:476
  2.4 0.0 copy-start
  2.4 1.4 %copy-done = s32[6,8,64,128]{3,2,1,0:T(8,128)S(1)} copy-done((s32[6,8,64,128]{3,2,1,0:T(8,128)S(1)}, s32[6,8,64,128]{3,2,1,0:T(8,128)}, u32[]{:S(2)}) %copy-start) | copy-done | bytes 1572888
  3.8 0.0 copy-start.1
  3.8 0.9 %copy-done.1 = f32[8,64,128]{2,1,0:T(8,128)S(1)} copy-done((f32[8,64,128]{2,1,0:T(8,128)S(1)}, f32[8,64,128]{2,1,0:T(8,128)}, u32[]{:S(2)}) %copy-start.1) | copy-done | bytes 262168
  4.8 0.0 copy-start.2
  4.8 0.9 %copy-done.2 = f32[8,64,128]{2,1,0:T(8,128)S(1)} copy-done((f32[8,64,128]{2,1,0:T(8,128)S(1)}, f32[8,64,128]{2,1,0:T(8,128)}, u32[]{:S(2)}) %copy-start.2) | copy-done | bytes 262168
  5.7 0.0 copy-start.5
  5.7 0.7 copy-done.5
  6.4 44.3 %evolve.1 = (f32[3,8,64,128]{3,2,1,0:T(8,128)S(1)}, f32[3,8,64,128]{3,2,1,0:T(8,128)S(1)}) custom-call(f32[8,64,128]{2,1,0:T(8,128)S(1)} %copy-done.1, f32[8,64,128]{2,1,0:T(8,128)S(1)} %copy-done.2, s32[6,8,64,128]{3,2,1,0:T(8,128)S(1)} %copy-done, f32[8]{0:T(128)S(1)} %copy-done.5), custom_call_target="tpu_custom_call" | custom-call | tf_op jit(solution)/shard_map/evolve/pallas_call | solution.py:342
  50.7 0.0 copy-done.3
  50.7 0.0 copy-done.4
  50.7 24.0 %modes.1 = f32[2,4,3,16,128]{4,3,2,1,0:T(8,128)S(1)} custom-call(f32[3,8,64,128]{3,2,1,0:T(8,128)S(1)} %get-tuple-element.6.mid_ref, f32[3,8,64,128]{3,2,1,0:T(8,128)S(1)} %get-tuple-element.12.end_ref, f32[64,64]{1,0:T(8,128)S(1)} %dynamic-slice_bitcast_fusion.1.x_ref, f32[512,128]{1,0:T(8,128)S(1)} %dynamic-slice_bitcast_fusion.y_ref, ...), custom_call_target="tpu_custom_call" | custom-call | tf_op jit(solution)/shard_map/modes/pallas_call | solution.py:482
  74.7 0.6 reshape.14
  75.4 0.4 fusion
  75.9 0.9 %squeeze.17 = f32[4,6144]{1,0:T(4,128)} reshape(f32[1,4,2,3,2,16,32]{6,5,4,3,2,1,0:T(8,128)S(1)} %copy.12) | data formatting | bytes 196608 | tf_op jit(solution)/shard_map/squeeze | solution.py:505
  76.7 0.9 %squeeze.16 = f32[4,6144]{1,0:T(4,128)} reshape(f32[1,4,2,3,2,16,32]{6,5,4,3,2,1,0:T(8,128)S(1)} %copy.11) | data formatting | bytes 196608 | tf_op jit(solution)/shard_map/squeeze | solution.py:505
  77.6 0.9 %copy.14 = f32[3,8,64,128]{3,2,1,0:T(8,128)} copy(f32[3,8,64,128]{3,2,1,0:T(8,128)S(1)} %get-tuple-element.12.end_ref) | data formatting | bytes 1572864
  (2 shorter events, 0.1 us)
Async XLA Ops:
  0.6 50.0 %copy-start.3 = (f32[16,16]{1,0:T(8,128)S(1)}, f32[16,16]{1,0:T(8,128)}, u32[]{:S(2)}) copy-start(f32[16,16]{1,0:T(8,128)} %constant.31.clone.sin_ref) | copy-start | bytes 3076
  0.6 50.0 %copy-start.4 = (f32[16,16]{1,0:T(8,128)S(1)}, f32[16,16]{1,0:T(8,128)}, u32[]{:S(2)}) copy-start(f32[16,16]{1,0:T(8,128)} %constant.30.clone.cos_ref) | copy-start | bytes 3076
  2.4 1.4 %copy-start = (s32[6,8,64,128]{3,2,1,0:T(8,128)S(1)}, s32[6,8,64,128]{3,2,1,0:T(8,128)}, u32[]{:S(2)}) copy-start(s32[6,8,64,128]{3,2,1,0:T(8,128)} %classes_ref.1) | copy-start | bytes 4718596
  3.8 0.9 %copy-start.1 = (f32[8,64,128]{2,1,0:T(8,128)S(1)}, f32[8,64,128]{2,1,0:T(8,128)}, u32[]{:S(2)}) copy-start(f32[8,64,128]{2,1,0:T(8,128)} %polar_ref.1) | copy-start | bytes 786436
  4.8 0.9 %copy-start.2 = (f32[8,64,128]{2,1,0:T(8,128)S(1)}, f32[8,64,128]{2,1,0:T(8,128)}, u32[]{:S(2)}) copy-start(f32[8,64,128]{2,1,0:T(8,128)} %azimuth_ref.1) | copy-start | bytes 786436
  5.7 0.7 copy-start.5

commit v2 on v1

--- a/solution.py
+++ b/solution.py
@@ -72,10 +72,10 @@
     )
 
 
-def evolve_kernel(sizes, polar_ref, azimuth_ref, classes_ref, table_ref, mid_ref, end_ref,
-                  S, Q, J, GS, GQ, GJ, OS, OQ, ins, low, high, lowk, highk,
+def evolve_kernel(sizes, polar_in, azimuth_in, classes_in, table_ref, mid_ref, end_ref,
+                  polar_ref, azimuth_ref, classes_ref, S, Q, J, GS, GQ, GJ, OS, OQ, ins, low, high, lowk, highk,
                   pack, left_pack, right_pack,
-                  xs, xr, ys, yr, zs, zr, gs, gr, osem):
+                  xs, xr, ys, yr, zs, zr, gs, gr, osem, isem):
     nx, ny, nz = sizes
     depth, wide, lanes = polar_ref.shape
     ext = wide + 2 * HALO
@@ -91,6 +91,13 @@
     y_left, y_right = at("gy", me_y, ny, -1), at("gy", me_y, ny, 1)
     z_down, z_up = at("gz", me_z, nz, -1), at("gz", me_z, nz, 1)
 
+    fetches = [
+        pltpu.make_async_copy(polar_in, polar_ref, isem.at[0]),
+        pltpu.make_async_copy(azimuth_in, azimuth_ref, isem.at[1]),
+        pltpu.make_async_copy(classes_in, classes_ref, isem.at[2]),
+    ]
+    for copy in fetches:
+        copy.start()
     barrier = pltpu.get_barrier_semaphore()
     for who in (x_left, x_right, y_left, y_right, z_down, z_up):
         pl.semaphore_signal(barrier, inc=1, device_id=who, device_id_type=MESH)
@@ -104,12 +111,12 @@
     top = pl.ds(wide - HALO, HALO)
     bottom = pl.ds(0, HALO)
     x_copies = [
-        remote(polar_ref.at[:, top, :], low.at[0], xs.at[0], xr.at[0], x_right),
-        remote(azimuth_ref.at[:, top, :], low.at[1], xs.at[1], xr.at[1], x_right),
-        remote(classes_ref.at[:, :, top, :], lowk, xs.at[2], xr.at[2], x_right),
-        remote(polar_ref.at[:, bottom, :], high.at[0], xs.at[3], xr.at[3], x_left),
-        remote(azimuth_ref.at[:, bottom, :], high.at[1], xs.at[4], xr.at[4], x_left),
-        remote(classes_ref.at[:, :, bottom, :], highk, xs.at[5], xr.at[5], x_left),
+        remote(polar_in.at[:, top, :], low.at[0], xs.at[0], xr.at[0], x_right),
+        remote(azimuth_in.at[:, top, :], low.at[1], xs.at[1], xr.at[1], x_right),
+        remote(classes_in.at[:, :, top, :], lowk, xs.at[2], xr.at[2], x_right),
+        remote(polar_in.at[:, bottom, :], high.at[0], xs.at[3], xr.at[3], x_left),
+        remote(azimuth_in.at[:, bottom, :], high.at[1], xs.at[4], xr.at[4], x_left),
+        remote(classes_in.at[:, :, bottom, :], highk, xs.at[5], xr.at[5], x_left),
     ]
     for copy in x_copies:
         copy.start()
@@ -142,6 +149,8 @@
                    lambda d: classes_ref[d, z, rows, :], HALO + 8 * r)
         return carry
 
+    for copy in fetches:
+        copy.wait()
     lax.fori_loop(0, depth, own, 0)
 
     def y_copies(part):
@@ -335,16 +344,17 @@
     ext = wide + 2 * HALO
     f32 = jnp.float32
     out = jax.ShapeDtypeStruct((3, depth, wide, lanes), f32)
-    vmem = pl.BlockSpec(memory_space=pltpu.VMEM)
+    hbm = pl.BlockSpec(memory_space=pltpu.HBM)
     anywhere = pl.BlockSpec(memory_space=pl.ANY)
     V = pltpu.VMEM
     D = pltpu.SemaphoreType.DMA
     return pl.pallas_call(
         functools.partial(evolve_kernel, sizes),
         out_shape=(out, out),
-        in_specs=[vmem, vmem, vmem, pl.BlockSpec(memory_space=pltpu.SMEM)],
+        in_specs=[hbm, hbm, hbm, pl.BlockSpec(memory_space=pltpu.SMEM)],
         out_specs=(anywhere, anywhere),
         scratch_shapes=[
+            V((depth, wide, lanes), f32), V((depth, wide, lanes), f32), V((6, depth, wide, lanes), jnp.int32),
             V((3, depth + 2, ext, lanes), f32), V((3, depth + 2, ext, lanes), f32),
             V((6, depth, ext, lanes), f32),
             V((3, ext, lanes), f32), V((3, ext, lanes), f32), V((6, ext, lanes), f32),
@@ -352,7 +362,7 @@
             V((2, depth, HALO, lanes), f32), V((2, depth, HALO, lanes), f32),
             V((6, depth, HALO, lanes), jnp.int32), V((6, depth, HALO, lanes), jnp.int32),
             V((9, ext, lanes), f32), V((9, ext, lanes), f32), V((9, ext, lanes), f32),
-            D((6,)), D((6,)), D((6,)), D((6,)), D((4,)), D((4,)), D((2,)), D((2,)), D((1,)),
+            D((6,)), D((6,)), D((6,)), D((6,)), D((4,)), D((4,)), D((2,)), D((2,)), D((1,)), D((3,)),
         ],
         compiler_params=pltpu.CompilerParams(collective_id=0, has_side_effects=True, vmem_limit_bytes=48 * 1024 * 1024),
         name="evolve",
@@ -369,16 +379,22 @@
     return jnp.dot(a, b, precision=lax.Precision.HIGHEST, preferred_element_type=jnp.float32)
 
 
-def modes_kernel(sizes, scale, mid_ref, end_ref, x_ref, y_ref, cos_ref, sin_ref, out_ref,
-                 T, R, Z, D, DR, E, F, zs, zr, xs, xr, ys, yr, fs, fr):
+def modes_kernel(sizes, scale, mid_ref, end_ref, x_in, y_in, cos_ref, sin_ref, out_ref,
+                 x_ref, y_ref, T, R, Z, D, DR, E, F, zs, zr, xs, xr, ys, yr, fs, fr, isem):
     nx, ny, nz = sizes
     depth, wide, lanes = mid_ref.shape[1:]
-    owned = D.shape[1]
+    owned = D.shape[2]
     half = KX // nz
     me_x, me_y, me_z = lax.axis_index("gx"), lax.axis_index("gy"), lax.axis_index("gz")
     peers_x = [{"gx": lax.rem(me_x + o, nx)} for o in range(1, nx)]
     peers_y = [{"gy": lax.rem(me_y + o, ny)} for o in range(1, ny)]
     twin = {"gz": 1 - me_z}
+    fetches = [
+        pltpu.make_async_copy(x_in.at[me_x], x_ref, isem.at[0]),
+        pltpu.make_async_copy(y_in.at[me_y], y_ref, isem.at[1]),
+    ]
+    for copy in fetches:
+        copy.start()
 
     barrier = pltpu.get_barrier_semaphore()
     for who in peers_x + peers_y + [twin]:
@@ -390,8 +406,14 @@
             src_ref=src, dst_ref=dst, send_sem=send, recv_sem=recv, device_id=who, device_id_type=MESH
         )
 
+    lane = lax.broadcasted_iota(jnp.int32, (half, 4 * KY), 1)
+    cosine_lane = (lane // KY) % 2 == 0
+    for copy in fetches:
+        copy.wait()
     table = x_ref[...]
-    for c in range(3):
+    swaps, x_copies, y_copies, shares = [], [], [], []
+
+    def transform(c):
         for z in range(depth):
             for turn, ref in enumerate((mid_ref, end_ref)):
                 along_x = exact_dot(table, ref[c, z])
@@ -400,20 +422,18 @@
         parts = exact_dot(T[...], y_ref[...]).reshape(depth, nz, half, 4 * KY)
         for h in range(nz):
             R[h, c] = parts[:, h]
-    swap = remote(R.at[1 - me_z], Z, zs.at[0], zr.at[0], twin)
-    swap.start()
-    swap.wait()
-
-    lane = lax.broadcasted_iota(jnp.int32, (half, 4 * KY), 1)
-    cosine_lane = (lane // KY) % 2 == 0
-
-    def waves(block, carry):
-        for c in range(3):
-            ones, twos = [], []
-            for z in range(nz * depth):
-                own = R[me_z, c, z] if z < depth else Z[c, z - depth]
-                ones.append(own)
-                twos.append(jnp.where(cosine_lane, -pltpu.roll(own, 3 * KY, 1), pltpu.roll(own, KY, 1)))
+        swaps.append(remote(R.at[1 - me_z, c], Z.at[c], zs.at[c], zr.at[c], twin))
+        swaps[c].start()
+
+    def waves(c):
+        swaps[c].wait()
+        ones, twos = [], []
+        for z in range(nz * depth):
+            own = R[me_z, c, z] if z < depth else Z[c, z - depth]
+            ones.append(own)
+            twos.append(jnp.where(cosine_lane, -pltpu.roll(own, 3 * KY, 1), pltpu.roll(own, KY, 1)))
+
+        def block_of(block, carry):
             for k in range(owned):
                 total = None
                 for z in range(nz * depth):
@@ -421,37 +441,56 @@
                     wave = block * owned + k
                     term = cos_ref[wave, where_z] * ones[z] + sin_ref[wave, where_z] * twos[z]
                     total = term if total is None else total + term
-                D[block, k, c] = total
-        return carry
-
-    lax.fori_loop(0, nx, waves, 0)
-    x_copies = [
-        remote(D.at[lax.rem(me_x + o, nx)], DR.at[o - 1], xs.at[o - 1], xr.at[o - 1], peers_x[o - 1])
-        for o in range(1, nx)
-    ]
-    for copy in x_copies:
-        copy.start()
-    for copy in x_copies:
-        copy.wait()
-    total = D[me_x]
-    for o in range(1, nx):
-        total = total + DR[o - 1]
-    E[me_y] = total
-    y_copies = [
-        remote(E.at[me_y], E.at[me_y], ys.at[o - 1], yr.at[o - 1], peers_y[o - 1]) for o in range(1, ny)
-    ]
-    for copy in y_copies:
-        copy.start()
-    for copy in y_copies:
-        copy.wait()
-    total = E[0]
-    for o in range(1, ny):
-        total = total + E[o]
-    F[me_z] = total * jnp.where(cosine_lane, scale, -scale)
-    share = remote(F.at[me_z], F.at[me_z], fs.at[0], fr.at[0], twin)
-    share.start()
-    share.wait()
-    out_ref[...] = F[...]
+                D[c, block, k] = total
+            return carry
+
+        lax.fori_loop(0, nx, block_of, 0)
+        x_copies.append([
+            remote(D.at[c, lax.rem(me_x + o, nx)], DR.at[c, o - 1], xs.at[c, o - 1], xr.at[c, o - 1], peers_x[o - 1])
+            for o in range(1, nx)
+        ])
+        for copy in reversed(x_copies[c]):
+            copy.start()
+
+    def sum_x(c):
+        for copy in x_copies[c]:
+            copy.wait()
+        total = D[c, me_x]
+        for o in range(1, nx):
+            total = total + DR[c, o - 1]
+        E[c, me_y] = total
+        y_copies.append([
+            remote(E.at[c, me_y], E.at[c, me_y], ys.at[c, o - 1], yr.at[c, o - 1], peers_y[o - 1])
+            for o in range(1, ny)
+        ])
+        for copy in y_copies[c]:
+            copy.start()
+
+    def sum_y(c):
+        for copy in y_copies[c]:
+            copy.wait()
+        total = E[c, 0]
+        for o in range(1, ny):
+            total = total + E[c, o]
+        F[c, me_z] = total * jnp.where(cosine_lane, scale, -scale)
+        shares.append(remote(F.at[c, me_z], F.at[c, me_z], fs.at[c], fr.at[c], twin))
+        shares[c].start()
+
+    transform(0)
+    transform(1)
+    waves(0)
+    transform(2)
+    waves(1)
+    waves(2)
+    sum_x(0)
+    sum_x(1)
+    sum_y(0)
+    sum_x(2)
+    sum_y(1)
+    sum_y(2)
+    for c in range(3):
+        shares[c].wait()
+        out_ref[:, :, c] = F[c]
 
 
 def modes(spin_mid, spin_end):
@@ -472,29 +511,29 @@
     y_full = np.zeros((ny, 4 * lanes, 4 * KY), np.float32)
     y_full[:, : 2 * lanes, : 2 * KY] = y_pair
     y_full[:, 2 * lanes :, 2 * KY :] = y_pair
-    x_table = lax.dynamic_index_in_dim(jnp.asarray(x_full), lax.axis_index("gx"), 0, False)
-    y_table = lax.dynamic_index_in_dim(jnp.asarray(y_full), lax.axis_index("gy"), 0, False)
     scale = float(wide * nx * lanes * ny * total_z) ** -0.5
     vmem = pl.BlockSpec(memory_space=pltpu.VMEM)
     smem = pl.BlockSpec(memory_space=pltpu.SMEM)
+    hbm = pl.BlockSpec(memory_space=pltpu.HBM)
     V, DMA = pltpu.VMEM, pltpu.SemaphoreType.DMA
     width = 4 * KY
     out = pl.pallas_call(
         functools.partial(modes_kernel, sizes, scale),
         out_shape=jax.ShapeDtypeStruct((nz, owned, 3, half, width), f32),
-        in_specs=[vmem, vmem, vmem, vmem, smem, smem],
+        in_specs=[vmem, vmem, hbm, hbm, smem, smem],
         out_specs=vmem,
         scratch_shapes=[
+            V((2 * KX, wide), f32), V((4 * lanes, width), f32),
             V((depth * KX, 4 * lanes), f32), V((nz, 3, depth, half, width), f32),
-            V((3, depth, half, width), f32), V((nx, owned, 3, half, width), f32),
-            V((nx - 1, owned, 3, half, width), f32), V((ny, owned, 3, half, width), f32),
-            V((nz, owned, 3, half, width), f32),
-            DMA((1,)), DMA((1,)), DMA((nx - 1,)), DMA((nx - 1,)), DMA((ny - 1,)), DMA((ny - 1,)),
-            DMA((1,)), DMA((1,)),
+            V((3, depth, half, width), f32), V((3, nx, owned, half, width), f32),
+            V((3, nx - 1, owned, half, width), f32), V((3, ny, owned, half, width), f32),
+            V((3, nz, owned, half, width), f32),
+            DMA((3,)), DMA((3,)), DMA((3, nx - 1)), DMA((3, nx - 1)), DMA((3, ny - 1)), DMA((3, ny - 1)),
+            DMA((3,)), DMA((3,)), DMA((2,)),
         ],
         compiler_params=pltpu.CompilerParams(collective_id=1, has_side_effects=True, vmem_limit_bytes=32 * 1024 * 1024),
         name="modes",
-    )(spin_mid, spin_end, x_table, y_table, jnp.asarray(z_cos.T), jnp.asarray(z_sin.T))
+    )(spin_mid, spin_end, jnp.asarray(x_full), jnp.asarray(y_full), jnp.asarray(z_cos.T), jnp.asarray(z_sin.T))
     out = out.reshape(nz, owned, 3, half, 2, 2, KY).transpose(4, 1, 5, 2, 0, 3, 6)
     return out.reshape(2, owned, -1)
 

time: 79 us -> 75.3 us (0.953)
  local copies, waits for them, and re-layouts: 9.42 us -> 7.68 us
  Pallas kernels: 68.3 us -> 66.7 us
    pallas_call x1, Pallas kernels: 24 us -> 22.2 us  [modes(): pl.pallas_call(functools.partial(modes_kernel, sizes, scale), out_shape=j...]
    squeeze x2 -> x0, local copies, waits for them, and re-layouts: 1.73 us -> none  [the longest x1 0.97 us: modes(): lax.dynamic_index_in_dim(jnp.asarray(y_full), lax.axis_index('gy'), 0, Fa...]
    unnamed x13 -> x17, local copies, waits for them, and re-layouts: 4.85 us -> 4.85 us
where the time goes in v2:
time: 75.3 us; the launch traced here: 75.1 us
  Pallas kernels  66.7 us (89%)
  local copies, waits for them, and re-layouts  7.68 us (10%)
    pallas_call x1, Pallas kernels, evolve(): pl.pallas_call(functools.partial(evolve_kernel, sizes), out_shape=(out, o...  44.5 us
    pallas_call x1, Pallas kernels, modes(): pl.pallas_call(functools.partial(modes_kernel, sizes, scale), out_shape=j...  22.2 us
    unnamed x17, local copies, waits for them, and re-layouts  4.85 us
    squeeze x2, local copies, waits for them, and re-layouts, body(): return (spin_end, both[0], both[1])  1.7 us

profile of v2, /device:TPU:0, one launch (start us, length us, event | category | flops | bytes accessed | tf_op | source)
XLA Modules:
  0.0 75.1 jit_solution(13796564902410370068)
XLA Ops:
  0.6 0.0 copy-start
  0.6 1.4 %copy-done = s32[6,8,64,128]{3,2,1,0:T(8,128)S(1)} copy-done((s32[6,8,64,128]{3,2,1,0:T(8,128)S(1)}, s32[6,8,64,128]{3,2,1,0:T(8,128)}, u32[]{:S(2)}) %copy-start) | copy-done | bytes 1572888
  2.0 0.0 copy-start.2
  2.0 0.9 %copy-done.2 = f32[8,64,128]{2,1,0:T(8,128)S(1)} copy-done((f32[8,64,128]{2,1,0:T(8,128)S(1)}, f32[8,64,128]{2,1,0:T(8,128)}, u32[]{:S(2)}) %copy-start.2) | copy-done | bytes 262168
  3.0 0.0 copy-start.3
  3.0 0.9 %copy-done.3 = f32[8,64,128]{2,1,0:T(8,128)S(1)} copy-done((f32[8,64,128]{2,1,0:T(8,128)S(1)}, f32[8,64,128]{2,1,0:T(8,128)}, u32[]{:S(2)}) %copy-start.3) | copy-done | bytes 262168
  3.9 0.0 copy-start.7
  3.9 0.7 copy-done.7
  4.6 0.0 copy-start.1
  4.6 0.0 copy-start.4
  4.6 0.0 copy-start.5
  4.6 0.0 copy-start.6
  4.6 44.5 %evolve.1 = (f32[3,8,64,128]{3,2,1,0:T(8,128)S(1)}, f32[3,8,64,128]{3,2,1,0:T(8,128)S(1)}) custom-call(f32[8,64,128]{2,1,0:T(8,128)S(1)} %copy-done.2, f32[8,64,128]{2,1,0:T(8,128)S(1)} %copy-done.3, s32[6,8,64,128]{3,2,1,0:T(8,128)S(1)} %copy-done, f32[8]{0:T(128)S(1)} %copy-done.7), custom_call_target="tpu_custom_call" | custom-call | tf_op jit(solution)/shard_map/evolve/pallas_call | solution.py:351
  49.1 0.0 copy-done.1
  49.1 0.0 copy-done.4
  49.1 0.0 copy-done.5
  49.1 0.0 copy-done.6
  49.1 22.2 %modes.1 = f32[2,4,3,16,128]{4,3,2,1,0:T(8,128)S(1)} custom-call(f32[3,8,64,128]{3,2,1,0:T(8,128)S(1)} %get-tuple-element.6.mid_ref, f32[3,8,64,128]{3,2,1,0:T(8,128)S(1)} %get-tuple-element.12.end_ref, f32[4,64,64]{2,1,0:T(8,128)S(1)} %copy-done.4, f32[2,512,128]{2,1,0:T(8,128)S(1)} %copy-done.1, f32[16,16]{1,0:T(8,128)S(1)} %copy-done.6, ...), custom_call_target="tpu_custom_call" | custom-call | tf_op jit(solution)/shard_map/modes/pallas_call | solution.py:520
  71.4 0.6 reshape.14
  72.0 0.4 fusion
  72.5 0.9 %squeeze.7 = f32[4,6144]{1,0:T(4,128)} reshape(f32[1,4,2,3,2,16,32]{6,5,4,3,2,1,0:T(8,128)S(1)} %copy.12) | data formatting | bytes 196608 | tf_op jit(solution)/shard_map/squeeze | solution.py:544
  73.4 0.9 %squeeze.6 = f32[4,6144]{1,0:T(4,128)} reshape(f32[1,4,2,3,2,16,32]{6,5,4,3,2,1,0:T(8,128)S(1)} %copy.11) | data formatting | bytes 196608 | tf_op jit(solution)/shard_map/squeeze | solution.py:544
  74.2 0.9 %copy.14 = f32[3,8,64,128]{3,2,1,0:T(8,128)} copy(f32[3,8,64,128]{3,2,1,0:T(8,128)S(1)} %get-tuple-element.12.end_ref) | data formatting | bytes 1572864
  (2 shorter events, 0.1 us)
Async XLA Ops:
  0.6 1.4 %copy-start = (s32[6,8,64,128]{3,2,1,0:T(8,128)S(1)}, s32[6,8,64,128]{3,2,1,0:T(8,128)}, u32[]{:S(2)}) copy-start(s32[6,8,64,128]{3,2,1,0:T(8,128)} %classes_in.1) | copy-start | bytes 4718596
  2.0 0.9 %copy-start.2 = (f32[8,64,128]{2,1,0:T(8,128)S(1)}, f32[8,64,128]{2,1,0:T(8,128)}, u32[]{:S(2)}) copy-start(f32[8,64,128]{2,1,0:T(8,128)} %polar_in.1) | copy-start | bytes 786436
  3.0 0.9 %copy-start.3 = (f32[8,64,128]{2,1,0:T(8,128)S(1)}, f32[8,64,128]{2,1,0:T(8,128)}, u32[]{:S(2)}) copy-start(f32[8,64,128]{2,1,0:T(8,128)} %azimuth_in.1) | copy-start | bytes 786436
  3.9 0.7 copy-start.7
  4.6 44.5 %copy-start.1 = (f32[2,512,128]{2,1,0:T(8,128)S(1)}, f32[2,512,128]{2,1,0:T(8,128)}, u32[]{:S(2)}) copy-start(f32[2,512,128]{2,1,0:T(8,128)} %constant.9.clone.y_in) | copy-start | bytes 1572868
  4.6 44.5 %copy-start.4 = (f32[4,64,64]{2,1,0:T(8,128)S(1)}, f32[4,64,64]{2,1,0:T(8,128)}, u32[]{:S(2)}) copy-start(f32[4,64,64]{2,1,0:T(8,128)} %constant.8.clone.x_in) | copy-start | bytes 196612
  4.6 44.5 %copy-start.5 = (f32[16,16]{1,0:T(8,128)S(1)}, f32[16,16]{1,0:T(8,128)}, u32[]{:S(2)}) copy-start(f32[16,16]{1,0:T(8,128)} %constant.11.clone.sin_ref) | copy-start | bytes 3076
  4.6 44.5 %copy-start.6 = (f32[16,16]{1,0:T(8,128)S(1)}, f32[16,16]{1,0:T(8,128)}, u32[]{:S(2)}) copy-start(f32[16,16]{1,0:T(8,128)} %constant.10.clone.cos_ref) | copy-start | bytes 3076

commit v3 on v2

--- a/solution.py
+++ b/solution.py
@@ -113,10 +113,14 @@
     x_copies = [
         remote(polar_in.at[:, top, :], low.at[0], xs.at[0], xr.at[0], x_right),
         remote(azimuth_in.at[:, top, :], low.at[1], xs.at[1], xr.at[1], x_right),
-        remote(classes_in.at[:, :, top, :], lowk, xs.at[2], xr.at[2], x_right),
+        remote(classes_in.at[pl.ds(0, 3), :, top, :], lowk.at[pl.ds(0, 3)], xs.at[2], xr.at[2], x_right),
+        remote(classes_in.at[4, :, top, :], lowk.at[4], xs.at[6], xr.at[6], x_right),
+        remote(classes_in.at[5, 0, top, :], lowk.at[5, 0], xs.at[7], xr.at[7], x_right),
         remote(polar_in.at[:, bottom, :], high.at[0], xs.at[3], xr.at[3], x_left),
         remote(azimuth_in.at[:, bottom, :], high.at[1], xs.at[4], xr.at[4], x_left),
-        remote(classes_in.at[:, :, bottom, :], highk, xs.at[5], xr.at[5], x_left),
+        remote(classes_in.at[pl.ds(0, 3), :, bottom, :], highk.at[pl.ds(0, 3)], xs.at[5], xr.at[5], x_left),
+        remote(classes_in.at[4, :, bottom, :], highk.at[4], xs.at[8], xr.at[8], x_left),
+        remote(classes_in.at[5, 0, bottom, :], highk.at[5, 0], xs.at[9], xr.at[9], x_left),
     ]
     for copy in x_copies:
         copy.start()
@@ -125,7 +129,7 @@
     group_of = lane // group
     place = lane % group
 
-    def spread(z, polar, azimuth, classes_at, row):
+    def spread(z, polar, azimuth, coupling_at, row):
         where_to = pl.ds(row, 8)
         shift = group * z + HALO
         mine = group_of == z
@@ -135,7 +139,7 @@
             old = pack[c, where_to, :]
             pack[c, where_to, :] = jnp.where(mine, pltpu.roll(spin[c], shift, 1), old)
         for d in range(6):
-            value = lookup(classes_at(d), table_ref)
+            value = coupling_at(d)
             J[d, z, where_to, :] = value
             old = pack[3 + d, where_to, :]
             pack[3 + d, where_to, :] = jnp.where(mine, pltpu.roll(value, shift, 1), old)
@@ -146,7 +150,7 @@
         for r in range(inner):
             rows = pl.ds(8 * r, 8)
             spread(z, polar_ref[z, rows, :], azimuth_ref[z, rows, :],
-                   lambda d: classes_ref[d, z, rows, :], HALO + 8 * r)
+                   lambda d: lookup(classes_ref[d, z, rows, :], table_ref), HALO + 8 * r)
         return carry
 
     for copy in fetches:
@@ -175,8 +179,18 @@
         copy.wait()
 
     def edges(z, carry):
-        spread(z, low[0, z], low[1, z], lambda d: lowk[d, z], 0)
-        spread(z, high[0, z], high[1, z], lambda d: highk[d, z], HALO + wide)
+        def coupling_at(halo, row, d):
+            if d == 3 and row > 0:
+                return J[0, z, pl.ds(row - 1, 8), :]
+            if d == 3:
+                return pltpu.roll(J[0, z, pl.ds(row, 8), :], 1, 0)
+            if d == 5:
+                below = J[2, jnp.maximum(z - 1, 0), pl.ds(row, 8), :]
+                return jnp.where(z == 0, lookup(halo[5, 0], table_ref), below)
+            return lookup(halo[d, z], table_ref)
+
+        spread(z, low[0, z], low[1, z], lambda d: coupling_at(lowk, 0, d), 0)
+        spread(z, high[0, z], high[1, z], lambda d: coupling_at(highk, HALO + wide, d), HALO + wide)
         return carry
 
     lax.fori_loop(0, depth, edges, 0)
@@ -362,9 +376,9 @@
             V((2, depth, HALO, lanes), f32), V((2, depth, HALO, lanes), f32),
             V((6, depth, HALO, lanes), jnp.int32), V((6, depth, HALO, lanes), jnp.int32),
             V((9, ext, lanes), f32), V((9, ext, lanes), f32), V((9, ext, lanes), f32),
-            D((6,)), D((6,)), D((6,)), D((6,)), D((4,)), D((4,)), D((2,)), D((2,)), D((1,)), D((3,)),
+            D((10,)), D((10,)), D((6,)), D((6,)), D((4,)), D((4,)), D((2,)), D((2,)), D((1,)), D((3,)),
         ],
-        compiler_params=pltpu.CompilerParams(collective_id=0, has_side_effects=True, vmem_limit_bytes=48 * 1024 * 1024),
+        compiler_params=pltpu.CompilerParams(collective_id=0, has_side_effects=True, vmem_limit_bytes=65200000),
         name="evolve",
     )(polar_angle, azimuth, classes, exchange_table)
 

time: 75.3 us -> 72.2 us (0.959)
  local copies, waits for them, and re-layouts: 7.68 us -> 6 us
  Pallas kernels: 66.7 us -> 65.2 us
    unnamed x17 -> x15, local copies, waits for them, and re-layouts: 4.85 us -> 3.17 us
    pallas_call x1, Pallas kernels: 44.5 us -> 43.1 us  [evolve(): pl.pallas_call(functools.partial(evolve_kernel, sizes), out_shape=(out, o...]
where the time goes in v3:
time: 72.2 us; the launch traced here: 72 us
  Pallas kernels  65.2 us (90%)
  local copies, waits for them, and re-layouts  6 us (8%)
  between operations  0.76 us (1%)
    pallas_call x1, Pallas kernels, evolve(): pl.pallas_call(functools.partial(evolve_kernel, sizes), out_shape=(out, o...  43.1 us
    pallas_call x1, Pallas kernels, modes(): pl.pallas_call(functools.partial(modes_kernel, sizes, scale), out_shape=j...  22.1 us
    unnamed x15, local copies, waits for them, and re-layouts  3.17 us
    squeeze x2, local copies, waits for them, and re-layouts, body(): return (spin_end, both[0], both[1])  1.7 us

profile of v3, /device:TPU:0, one launch (start us, length us, event | category | flops | bytes accessed | tf_op | source)
XLA Modules:
  0.0 72.0 jit_solution(222464935238934042)
XLA Ops:
  0.6 0.0 copy-start.5
  0.6 0.0 copy-start.6
  0.7 0.0 copy-start.3
  0.7 0.0 copy-start.4
  0.7 43.1 %evolve.1 = (f32[3,8,64,128]{3,2,1,0:T(8,128)}, f32[3,8,64,128]{3,2,1,0:T(8,128)}) custom-call(f32[8,64,128]{2,1,0:T(8,128)} %polar_in.1, f32[8,64,128]{2,1,0:T(8,128)} %azimuth_in.1, s32[6,8,64,128]{3,2,1,0:T(8,128)} %classes_in.1, f32[8]{0:T(128)} %table_ref.1), custom_call_target="tpu_custom_call" | custom-call | tf_op jit(solution)/shard_map/evolve/pallas_call | solution.py:365
  43.8 0.0 copy-done.5
  43.8 0.0 copy-done.6
  43.8 0.0 copy-done.3
  43.8 0.0 copy-done.4
  43.8 0.0 copy-start
  43.8 1.1 %copy-done = f32[3,8,64,128]{3,2,1,0:T(8,128)S(1)} copy-done((f32[3,8,64,128]{3,2,1,0:T(8,128)S(1)}, f32[3,8,64,128]{3,2,1,0:T(8,128)}, u32[]{:S(2)}) %copy-start) | copy-done | bytes 786456
  45.0 0.0 copy-start.2
  45.0 1.1 %copy-done.2 = f32[3,8,64,128]{3,2,1,0:T(8,128)S(1)} copy-done((f32[3,8,64,128]{3,2,1,0:T(8,128)S(1)}, f32[3,8,64,128]{3,2,1,0:T(8,128)}, u32[]{:S(2)}) %copy-start.2) | copy-done | bytes 786456
  46.1 22.1 %modes.1 = f32[2,4,3,16,128]{4,3,2,1,0:T(8,128)S(1)} custom-call(f32[3,8,64,128]{3,2,1,0:T(8,128)S(1)} %copy-done.2, f32[3,8,64,128]{3,2,1,0:T(8,128)S(1)} %copy-done, f32[4,64,64]{2,1,0:T(8,128)S(1)} %copy-done.4, f32[2,512,128]{2,1,0:T(8,128)S(1)} %copy-done.3, f32[16,16]{1,0:T(8,128)S(1)} %copy-done.6, f32[16,16]{1,0:T(8,128)S(1)} %copy-done.5), custom_call_target="tpu_custom_call" | custom-call | tf_op jit(solution)/shard_map/modes/pallas_call | solution.py:534
  68.2 0.6 reshape.14
  68.9 0.4 fusion
  69.3 0.0 copy-start.1
  69.4 0.9 %squeeze.7 = f32[4,6144]{1,0:T(4,128)} reshape(f32[1,4,2,3,2,16,32]{6,5,4,3,2,1,0:T(8,128)S(1)} %copy.12) | data formatting | bytes 196608 | tf_op jit(solution)/shard_map/squeeze | solution.py:558
  70.2 0.9 %squeeze.6 = f32[4,6144]{1,0:T(4,128)} reshape(f32[1,4,2,3,2,16,32]{6,5,4,3,2,1,0:T(8,128)S(1)} %copy.11) | data formatting | bytes 196608 | tf_op jit(solution)/shard_map/squeeze | solution.py:558
  71.1 0.0 copy-done.1
  71.1 0.9 %copy.14 = f32[3,8,64,128]{3,2,1,0:T(8,128)} copy(f32[3,8,64,128]{3,2,1,0:T(8,128)S(1)} %copy-done.1) | data formatting | bytes 1572864
  (2 shorter events, 0.1 us)
Async XLA Ops:
  0.6 43.2 %copy-start.5 = (f32[16,16]{1,0:T(8,128)S(1)}, f32[16,16]{1,0:T(8,128)}, u32[]{:S(2)}) copy-start(f32[16,16]{1,0:T(8,128)} %constant.11.clone.sin_ref) | copy-start | bytes 3076
  0.6 43.2 %copy-start.6 = (f32[16,16]{1,0:T(8,128)S(1)}, f32[16,16]{1,0:T(8,128)}, u32[]{:S(2)}) copy-start(f32[16,16]{1,0:T(8,128)} %constant.10.clone.cos_ref) | copy-start | bytes 3076
  0.7 43.2 %copy-start.3 = (f32[2,512,128]{2,1,0:T(8,128)S(1)}, f32[2,512,128]{2,1,0:T(8,128)}, u32[]{:S(2)}) copy-start(f32[2,512,128]{2,1,0:T(8,128)} %constant.9.clone.y_in) | copy-start | bytes 1572868
  0.7 43.2 %copy-start.4 = (f32[4,64,64]{2,1,0:T(8,128)S(1)}, f32[4,64,64]{2,1,0:T(8,128)}, u32[]{:S(2)}) copy-start(f32[4,64,64]{2,1,0:T(8,128)} %constant.8.clone.x_in) | copy-start | bytes 196612
  43.8 1.1 %copy-start = (f32[3,8,64,128]{3,2,1,0:T(8,128)S(1)}, f32[3,8,64,128]{3,2,1,0:T(8,128)}, u32[]{:S(2)}) copy-start(f32[3,8,64,128]{3,2,1,0:T(8,128)} %get-tuple-element.12.end_ref) | copy-start | bytes 2359300
  45.0 1.1 %copy-start.2 = (f32[3,8,64,128]{3,2,1,0:T(8,128)S(1)}, f32[3,8,64,128]{3,2,1,0:T(8,128)}, u32[]{:S(2)}) copy-start(f32[3,8,64,128]{3,2,1,0:T(8,128)} %get-tuple-element.6.mid_ref) | copy-start | bytes 2359300
  69.3 1.8 %copy-start.1 = (f32[3,8,64,128]{3,2,1,0:T(8,128)S(1)}, f32[3,8,64,128]{3,2,1,0:T(8,128)}, u32[]{:S(2)}) copy-start(f32[3,8,64,128]{3,2,1,0:T(8,128)} %get-tuple-element.12.end_ref) | copy-start | bytes 2359300
